TPU v7x, 32 devices: a whole 2x2x4 slice. The times are simulated.
32 devices in a mesh: prow: 8 (over y, x, core), pcol: 4 (over z).
Axes of the slice: x: 2, y: 2, z: 4, core: 2. Of those that a mesh axis runs over, the one named last changes fastest.
Arguments:
- panel: float32 [16, 1024, 128], P('pcol', 'prow'), may hold values from -8 to 192, as said below
- strip: float32 [16, 1024, 2, 512], P(None, 'prow', None, 'pcol'), may hold values from -6 to 6
- factor: float32 [16, 1024, 2, 512], P(None, 'prow', None, 'pcol'), may hold values from -0.125 to 0.125
- inv_diag: float32 [8, 128, 128], replicated, may hold values from -0.24 to 1.4, as said below
- rhs: float32 [16, 1024, 256], P(None, 'prow'), may hold values from -6 to 6
Outputs:
- panel_factor: float32 [16, 1024, 128], P('pcol', 'prow')
- new_strip: float32 [16, 1024, 2, 512], P(None, 'prow', None, 'pcol')
- forward: float32 [16, 1024, 256], P(None, 'prow')
Inputs may be any that keep to these rules, and one draw needn't show every extreme that they name: Row tile 8 of the panel, read as in the first step, is symmetric positive definite. `inv_diag`: every block is lower triangular with a positive diagonal.
All inputs are finite; a program needn't handle non-finite values.
Results may differ from a plain program's by a relative error of at most 0.00018.
Values sent between devices are 32-bit elements; how exact they have to be, the bound alone decides.
A program may use at most 64 MiB of HBM per device.

v0:
```python
import jax
import jax.numpy as jnp
from jax import lax
from jax.sharding import PartitionSpec as P

KF = 2
CTD = 2


def from_root(block, axis, owner):
    block = jnp.where(lax.axis_index(axis) == owner, block, jnp.zeros_like(block))
    return lax.psum(block, axis)


def per_device(panel, strip, factor, inv_diag, rhs):
    highest = lax.Precision.HIGHEST
    grid_rows = lax.axis_size("prow")
    grid_cols = lax.axis_size("pcol")
    row_place = lax.axis_index("prow")
    col_place = lax.axis_index("pcol")
    own_tiles = panel.shape[0]
    tile_size = panel.shape[1]
    tile_rows = strip.shape[0]
    rhs_count = rhs.shape[2]
    sweep_tiles = KF * grid_cols
    strip_tiles = CTD * grid_cols
    diag_row = sweep_tiles // grid_rows
    root_index = sweep_tiles % grid_rows * grid_cols + diag_row // own_tiles
    diag_block = from_root(panel[diag_row % own_tiles], ("prow", "pcol"), root_index)
    diag_factor = jnp.linalg.cholesky(diag_block)
    inverse = jax.scipy.linalg.solve_triangular(
        diag_factor, jnp.eye(tile_size, dtype=jnp.float32), lower=True
    )
    scaled = jnp.einsum("atb,cb->atc", panel, inverse, precision=highest)
    local_tile = (col_place * own_tiles + jnp.arange(own_tiles)) * grid_rows + row_place
    panel_factor = jnp.where((local_tile > sweep_tiles)[:, None, None], scaled, 0.0)
    panel_factor = jnp.where(
        (local_tile == sweep_tiles)[:, None, None], diag_factor[None], panel_factor
    )
    row_factor = lax.all_gather(panel_factor, "pcol", axis=0, tiled=True)
    row_tile = jnp.arange(tile_rows) * grid_rows + row_place
    below_part = jnp.where((row_tile > sweep_tiles)[:, None, None], row_factor, 0.0)
    wanted = sweep_tiles + 1 + jnp.arange(CTD) * grid_cols + col_place
    slot_count = -(-strip_tiles // grid_rows)
    first_slot = (sweep_tiles + grid_rows - row_place) // grid_rows
    outgoing = lax.dynamic_slice_in_dim(below_part, first_slot, slot_count, 0)
    pooled = lax.all_gather(outgoing, "prow", axis=0, tiled=True)
    owner_row = wanted % grid_rows
    slot_place = (
        owner_row * slot_count
        + wanted // grid_rows
        - (sweep_tiles + grid_rows - owner_row) // grid_rows
    )
    column = pooled[slot_place]
    new_strip = strip - jnp.einsum("itb,scb->itsc", below_part, column, precision=highest)
    start_solved = jnp.zeros((sweep_tiles, tile_size, rhs_count), jnp.float32)
    reduce_row = lambda pending: lax.psum(pending, "pcol")
    spread_row = lambda solution, root_row: from_root(solution, "prow", root_row)

    def advance(sweep_step, carried):
        partial_rows, solved, pending = carried
        tile_here = sweep_step // grid_rows
        pending = lax.dynamic_index_in_dim(partial_rows, tile_here, 0, keepdims=False)
        summed = reduce_row(pending)
        residue = lax.dynamic_index_in_dim(rhs, tile_here, 0, keepdims=False) - summed
        diag_inverse = lax.dynamic_index_in_dim(inv_diag, sweep_step, 0, keepdims=False)
        solution = jnp.dot(diag_inverse, residue, precision=highest)
        solution = spread_row(solution, sweep_step % grid_rows)
        solved = lax.dynamic_update_index_in_dim(solved, solution, sweep_step, 0)
        columns = lax.dynamic_index_in_dim(factor, sweep_step // grid_cols, 2, keepdims=False)
        holds_column = col_place == sweep_step % grid_cols
        update = jnp.einsum("itc,cr->itr", columns, solution, precision=highest)
        partial_rows = partial_rows + jnp.where(holds_column, update, 0.0)
        return (partial_rows, solved, pending)

    start_rows = jnp.zeros(rhs.shape, jnp.float32)
    start_pending = jnp.zeros((tile_size, rhs_count), jnp.float32)
    partial_rows, solved, unused_pending = lax.fori_loop(
        0, sweep_tiles, advance, (start_rows, start_solved, start_pending)
    )
    partial_rows, solved = (partial_rows, solved)
    totals = lax.psum(partial_rows, "pcol")
    remains = rhs - totals
    panel_solution = jnp.dot(inverse, remains[sweep_tiles // grid_rows], precision=highest)
    panel_solution = from_root(panel_solution, "prow", sweep_tiles % grid_rows)
    remains = remains - jnp.einsum("itb,br->itr", below_part, panel_solution, precision=highest)
    earlier = solved[jnp.minimum(row_tile, sweep_tiles - 1)]
    forward = jnp.where((row_tile == sweep_tiles)[:, None, None], panel_solution[None], remains)
    forward = jnp.where((row_tile < sweep_tiles)[:, None, None], earlier, forward)
    return (panel_factor, new_strip, forward)


def solution(mesh):
    in_specs = (
        P("pcol", "prow", None),
        P(None, "prow", None, "pcol"),
        P(None, "prow", None, "pcol"),
        P(),
        P(None, "prow", None),
    )
    out_specs = (P("pcol", "prow", None), P(None, "prow", None, "pcol"), P(None, "prow", None))
    return jax.shard_map(
        per_device, mesh=mesh, in_specs=in_specs, out_specs=out_specs, check_vma=False
    )
```

profile of v0, /device:TPU:0, one launch (start us, length us, event | category | flops | bytes accessed | tf_op | source)
XLA Modules:
  0.0 1144.2 jit_solution(4040450262911026411)
XLA Ops:
  8.9 125.6 %all-reduce.6.cloned.1.call-done = f32[128,128]{0,1:T(8,128)} async-done(((f32[128,128]{0,1:T(8,128)}), f32[128,128]{0,1:T(8,128)}) %all-reduce.6.cloned.1.call-update) | async-done | bytes 65552 | tf_op jit(solution)/shard_map/psum | solution.py:12
  136.2 11.7 %cholesky.19 = f32[128,128]{1,0:T(8,128)S(1)} custom-call(f32[128,128]{1,0:T(8,128)S(1)} %fusion.13), custom_call_target="Cholesky" | custom-call | tf_op jit(solution)/shard_map/jit(cholesky)/cholesky | solution.py:30
  149.3 9.8 custom-call.7
  161.6 796.4 %while.19 = (s32[]{:T(128)}, f32[16,128,256]{2,1,0:T(8,128)}, f32[8,128,256]{2,1,0:T(8,128)}, s32[]{:T(128)}, f32[16,128,2,128]{3,2,1,0:T(2,128)}, /*index=5*/f3...) while((s32[]{:T(128)}, f32[16,128,256]{2,1,0:T(8,128)}, ...), condition=%wide.region_6.7_spmd.clone, body=%wide.region_3.6_spmd.clone.sunk | while | flops 857342016 | bytes 14221928 | solution.py:78
  162.6 38.0 %all-reduce.12.cloned.1.call-done = f32[128,256]{1,0:T(8,128)} async-done(((f32[128,256]{1,0:T(8,128)}), f32[128,256]{1,0:T(8,128)}) %all-reduce.12.cloned.1.call-update) | async-done | bytes 131088 | tf_op jit(solution)/shard_map/while/body/eval_jaxpr/psum | solution.py:57
  200.7 1.9 convolution_select_fusion.4
  202.6 2.7 constant_dynamic-slice_fusion.3
  205.3 51.9 %all-reduce.14.cloned.1.call-done = f32[128,256]{1,0:T(8,128)} async-done(((f32[128,256]{1,0:T(8,128)}), f32[128,256]{1,0:T(8,128)}) %all-reduce.14.cloned.1.call-update) | async-done | bytes 131088 | tf_op jit(solution)/shard_map/while/body/eval_jaxpr/psum | solution.py:12
  257.2 1.6 bitcast_dynamic-update-slice_fusion.2
  258.7 4.0 select_add_fusion.2
  262.7 1.8 broadcast_select_fusion.3
  265.3 34.7 %all-reduce.12.cloned.1.call-done = f32[128,256]{1,0:T(8,128)} async-done(((f32[128,256]{1,0:T(8,128)}), f32[128,256]{1,0:T(8,128)}) %all-reduce.12.cloned.1.call-update) | async-done | bytes 131088 | tf_op jit(solution)/shard_map/while/body/eval_jaxpr/psum | solution.py:57
  300.0 1.9 convolution_select_fusion.4
  302.0 2.7 constant_dynamic-slice_fusion.3
  304.7 51.7 %all-reduce.14.cloned.1.call-done = f32[128,256]{1,0:T(8,128)} async-done(((f32[128,256]{1,0:T(8,128)}), f32[128,256]{1,0:T(8,128)}) %all-reduce.14.cloned.1.call-update) | async-done | bytes 131088 | tf_op jit(solution)/shard_map/while/body/eval_jaxpr/psum | solution.py:12
  356.4 1.6 bitcast_dynamic-update-slice_fusion.2
  357.9 4.0 select_add_fusion.2
  361.9 1.8 broadcast_select_fusion.3
  364.5 34.7 %all-reduce.12.cloned.1.call-done = f32[128,256]{1,0:T(8,128)} async-done(((f32[128,256]{1,0:T(8,128)}), f32[128,256]{1,0:T(8,128)}) %all-reduce.12.cloned.1.call-update) | async-done | bytes 131088 | tf_op jit(solution)/shard_map/while/body/eval_jaxpr/psum | solution.py:57
  399.2 1.9 convolution_select_fusion.4
  401.2 2.7 constant_dynamic-slice_fusion.3
  403.9 51.9 %all-reduce.14.cloned.1.call-done = f32[128,256]{1,0:T(8,128)} async-done(((f32[128,256]{1,0:T(8,128)}), f32[128,256]{1,0:T(8,128)}) %all-reduce.14.cloned.1.call-update) | async-done | bytes 131088 | tf_op jit(solution)/shard_map/while/body/eval_jaxpr/psum | solution.py:12
  455.7 1.6 bitcast_dynamic-update-slice_fusion.2
  457.3 4.0 select_add_fusion.2
  461.3 1.8 broadcast_select_fusion.3
  463.9 35.0 %all-reduce.12.cloned.1.call-done = f32[128,256]{1,0:T(8,128)} async-done(((f32[128,256]{1,0:T(8,128)}), f32[128,256]{1,0:T(8,128)}) %all-reduce.12.cloned.1.call-update) | async-done | bytes 131088 | tf_op jit(solution)/shard_map/while/body/eval_jaxpr/psum | solution.py:57
  498.9 1.9 convolution_select_fusion.4
  500.8 2.7 constant_dynamic-slice_fusion.3
  503.5 51.9 %all-reduce.14.cloned.1.call-done = f32[128,256]{1,0:T(8,128)} async-done(((f32[128,256]{1,0:T(8,128)}), f32[128,256]{1,0:T(8,128)}) %all-reduce.14.cloned.1.call-update) | async-done | bytes 131088 | tf_op jit(solution)/shard_map/while/body/eval_jaxpr/psum | solution.py:12
  557.0 4.0 select_add_fusion.2
  561.0 1.8 broadcast_select_fusion.3
  563.6 34.6 %all-reduce.12.cloned.1.call-done = f32[128,256]{1,0:T(8,128)} async-done(((f32[128,256]{1,0:T(8,128)}), f32[128,256]{1,0:T(8,128)}) %all-reduce.12.cloned.1.call-update) | async-done | bytes 131088 | tf_op jit(solution)/shard_map/while/body/eval_jaxpr/psum | solution.py:57
  598.2 1.9 convolution_select_fusion.4
  600.1 2.7 constant_dynamic-slice_fusion.3
  602.8 51.9 %all-reduce.14.cloned.1.call-done = f32[128,256]{1,0:T(8,128)} async-done(((f32[128,256]{1,0:T(8,128)}), f32[128,256]{1,0:T(8,128)}) %all-reduce.14.cloned.1.call-update) | async-done | bytes 131088 | tf_op jit(solution)/shard_map/while/body/eval_jaxpr/psum | solution.py:12
  656.3 4.0 select_add_fusion.2
  660.3 1.8 broadcast_select_fusion.3
  662.9 34.7 %all-reduce.12.cloned.1.call-done = f32[128,256]{1,0:T(8,128)} async-done(((f32[128,256]{1,0:T(8,128)}), f32[128,256]{1,0:T(8,128)}) %all-reduce.12.cloned.1.call-update) | async-done | bytes 131088 | tf_op jit(solution)/shard_map/while/body/eval_jaxpr/psum | solution.py:57
  697.6 1.9 convolution_select_fusion.4
  699.5 2.7 constant_dynamic-slice_fusion.3
  702.2 51.9 %all-reduce.14.cloned.1.call-done = f32[128,256]{1,0:T(8,128)} async-done(((f32[128,256]{1,0:T(8,128)}), f32[128,256]{1,0:T(8,128)}) %all-reduce.14.cloned.1.call-update) | async-done | bytes 131088 | tf_op jit(solution)/shard_map/while/body/eval_jaxpr/psum | solution.py:12
  755.6 4.0 select_add_fusion.2
  759.6 1.8 broadcast_select_fusion.3
  762.2 34.6 %all-reduce.12.cloned.1.call-done = f32[128,256]{1,0:T(8,128)} async-done(((f32[128,256]{1,0:T(8,128)}), f32[128,256]{1,0:T(8,128)}) %all-reduce.12.cloned.1.call-update) | async-done | bytes 131088 | tf_op jit(solution)/shard_map/while/body/eval_jaxpr/psum | solution.py:57
  796.9 1.9 convolution_select_fusion.4
  798.8 2.7 constant_dynamic-slice_fusion.3
  801.5 51.7 %all-reduce.14.cloned.1.call-done = f32[128,256]{1,0:T(8,128)} async-done(((f32[128,256]{1,0:T(8,128)}), f32[128,256]{1,0:T(8,128)}) %all-reduce.14.cloned.1.call-update) | async-done | bytes 131088 | tf_op jit(solution)/shard_map/while/body/eval_jaxpr/psum | solution.py:12
  854.8 4.0 select_add_fusion.2
  858.8 1.8 broadcast_select_fusion.3
  861.4 34.7 %all-reduce.12.cloned.1.call-done = f32[128,256]{1,0:T(8,128)} async-done(((f32[128,256]{1,0:T(8,128)}), f32[128,256]{1,0:T(8,128)}) %all-reduce.12.cloned.1.call-update) | async-done | bytes 131088 | tf_op jit(solution)/shard_map/while/body/eval_jaxpr/psum | solution.py:57
  896.1 1.9 convolution_select_fusion.4
  898.0 2.7 constant_dynamic-slice_fusion.3
  900.7 51.7 %all-reduce.14.cloned.1.call-done = f32[128,256]{1,0:T(8,128)} async-done(((f32[128,256]{1,0:T(8,128)}), f32[128,256]{1,0:T(8,128)}) %all-reduce.14.cloned.1.call-update) | async-done | bytes 131088 | tf_op jit(solution)/shard_map/while/body/eval_jaxpr/psum | solution.py:12
  952.4 1.6 bitcast_dynamic-update-slice_fusion.2
  954.0 4.0 select_add_fusion.2
  959.4 2.0 gather_fusion.1
  961.5 26.5 %all-gather.2.cloned.1.call-done = f32[16,128,128]{2,1,0:T(8,128)} async-done(((f32[4,128,128]{2,1,0:T(8,128)}), f32[16,128,128]{2,1,0:T(8,128)}) %all-gather.2.cloned.1.call-update) | async-done | bytes 1048592 | tf_op jit(solution)/shard_map/all_gather | solution.py:40
  989.4 10.0 all_gather.7
  1000.0 77.0 %all-reduce.8.cloned.1.call-done = f32[16,128,256]{2,1,0:T(8,128)} async-done(((f32[16,128,256]{2,1,0:T(8,128)}), f32[16,128,256]{2,1,0:T(8,128)}) %all-reduce.8.cloned.1.call-update) | async-done | bytes 2097168 | tf_op jit(solution)/shard_map/psum | solution.py:82
  1077.0 2.5 sub.72
  1080.5 3.4 copy_subtract_fusion
  1083.9 2.9 copy.25
  1086.8 45.9 %all-reduce.10.cloned.1.call-done = f32[128,256]{1,0:T(8,128)} async-done(((f32[128,256]{1,0:T(8,128)}), f32[128,256]{1,0:T(8,128)}) %all-reduce.10.cloned.1.call-update) | async-done | bytes 131088 | tf_op jit(solution)/shard_map/psum | solution.py:12
  1132.7 4.7 select_select_fusion
  (80 shorter events, 24.0 us)
Async XLA Ops:
  7.2 127.3 %all-reduce.6.cloned.1.call-start = ((), (), s32[]{:S(2)}) async-start(), calls=%async_computation | async-start | bytes 131072 | tf_op jit(solution)/shard_map/psum | solution.py:12
  161.6 39.0 %all-reduce.12.cloned.1.call-start = ((), (), s32[]{:S(2)}) async-start(), calls=%async_computation.4 | async-start | bytes 262144 | tf_op jit(solution)/shard_map/while/body/eval_jaxpr/psum | solution.py:57
  162.6 94.6 %all-reduce.14.cloned.1.call-start = ((), (), s32[]{:S(2)}) async-start(), calls=%async_computation.5 | async-start | bytes 262144 | tf_op jit(solution)/shard_map/while/body/eval_jaxpr/psum | solution.py:12
  262.7 37.3 %all-reduce.12.cloned.1.call-start = ((), (), s32[]{:S(2)}) async-start(), calls=%async_computation.4 | async-start | bytes 262144 | tf_op jit(solution)/shard_map/while/body/eval_jaxpr/psum | solution.py:57
  265.3 91.1 %all-reduce.14.cloned.1.call-start = ((), (), s32[]{:S(2)}) async-start(), calls=%async_computation.5 | async-start | bytes 262144 | tf_op jit(solution)/shard_map/while/body/eval_jaxpr/psum | solution.py:12
  361.9 37.3 %all-reduce.12.cloned.1.call-start = ((), (), s32[]{:S(2)}) async-start(), calls=%async_computation.4 | async-start | bytes 262144 | tf_op jit(solution)/shard_map/while/body/eval_jaxpr/psum | solution.py:57
  364.5 91.3 %all-reduce.14.cloned.1.call-start = ((), (), s32[]{:S(2)}) async-start(), calls=%async_computation.5 | async-start | bytes 262144 | tf_op jit(solution)/shard_map/while/body/eval_jaxpr/psum | solution.py:12
  461.3 37.5 %all-reduce.12.cloned.1.call-start = ((), (), s32[]{:S(2)}) async-start(), calls=%async_computation.4 | async-start | bytes 262144 | tf_op jit(solution)/shard_map/while/body/eval_jaxpr/psum | solution.py:57
  463.8 91.6 %all-reduce.14.cloned.1.call-start = ((), (), s32[]{:S(2)}) async-start(), calls=%async_computation.5 | async-start | bytes 262144 | tf_op jit(solution)/shard_map/while/body/eval_jaxpr/psum | solution.py:12
  561.0 37.2 %all-reduce.12.cloned.1.call-start = ((), (), s32[]{:S(2)}) async-start(), calls=%async_computation.4 | async-start | bytes 262144 | tf_op jit(solution)/shard_map/while/body/eval_jaxpr/psum | solution.py:57
  563.5 91.2 %all-reduce.14.cloned.1.call-start = ((), (), s32[]{:S(2)}) async-start(), calls=%async_computation.5 | async-start | bytes 262144 | tf_op jit(solution)/shard_map/while/body/eval_jaxpr/psum | solution.py:12
  660.3 37.3 %all-reduce.12.cloned.1.call-start = ((), (), s32[]{:S(2)}) async-start(), calls=%async_computation.4 | async-start | bytes 262144 | tf_op jit(solution)/shard_map/while/body/eval_jaxpr/psum | solution.py:57
  662.8 91.3 %all-reduce.14.cloned.1.call-start = ((), (), s32[]{:S(2)}) async-start(), calls=%async_computation.5 | async-start | bytes 262144 | tf_op jit(solution)/shard_map/while/body/eval_jaxpr/psum | solution.py:12
  759.6 37.2 %all-reduce.12.cloned.1.call-start = ((), (), s32[]{:S(2)}) async-start(), calls=%async_computation.4 | async-start | bytes 262144 | tf_op jit(solution)/shard_map/while/body/eval_jaxpr/psum | solution.py:57
  762.2 91.1 %all-reduce.14.cloned.1.call-start = ((), (), s32[]{:S(2)}) async-start(), calls=%async_computation.5 | async-start | bytes 262144 | tf_op jit(solution)/shard_map/while/body/eval_jaxpr/psum | solution.py:12
  858.8 37.3 %all-reduce.12.cloned.1.call-start = ((), (), s32[]{:S(2)}) async-start(), calls=%async_computation.4 | async-start | bytes 262144 | tf_op jit(solution)/shard_map/while/body/eval_jaxpr/psum | solution.py:57
  861.3 91.1 %all-reduce.14.cloned.1.call-start = ((), (), s32[]{:S(2)}) async-start(), calls=%async_computation.5 | async-start | bytes 262144 | tf_op jit(solution)/shard_map/while/body/eval_jaxpr/psum | solution.py:12
  958.0 1.4 copy-start
  958.0 30.0 %all-gather.2.cloned.1.call-start = ((), (), s32[]{:S(2)}) async-start(), calls=%async_computation.1 | async-start | bytes 1310720 | tf_op jit(solution)/shard_map/all_gather | solution.py:40
  958.6 118.4 %all-reduce.8.cloned.1.call-start = ((), (), s32[]{:S(2)}) async-start(), calls=%async_computation.2 | async-start | bytes 4194304 | tf_op jit(solution)/shard_map/psum | solution.py:82
  959.3 173.4 %all-reduce.10.cloned.1.call-start = ((), (), s32[]{:S(2)}) async-start(), calls=%async_computation.3 | async-start | bytes 262144 | tf_op jit(solution)/shard_map/psum | solution.py:12
Sparse Core Ops, SparseCore 0:
  14.2 120.2 all-reduce.5
  165.4 35.2 all-reduce.11
  204.6 52.5 all-reduce.13
  266.1 33.8 all-reduce.11
  303.8 52.5 all-reduce.13
  365.3 33.8 all-reduce.11
  403.1 52.5 all-reduce.13
  465.0 33.7 all-reduce.11
  502.8 52.5 all-reduce.13
  564.4 33.7 all-reduce.11
  602.1 52.5 all-reduce.13
  663.7 33.8 all-reduce.11
  701.5 52.5 all-reduce.13
  763.0 33.7 all-reduce.11
  800.6 52.5 all-reduce.13
  862.2 33.8 all-reduce.11
  899.8 52.5 all-reduce.13
  960.7 27.2 all-gather.1
  990.9 86.0 all-reduce.7
  1080.7 51.9 all-reduce.9
where the time goes:
time: 1150 us; the launch traced here: 1140 us
  waiting for transfers between devices  972 us (85%)
  matrix products  58 us (5%)
  local copies, waits for them, and re-layouts  47.7 us (4%)
  other arithmetic  41.2 us (4%)
  between operations  14.2 us (1%)
    psum x10, waiting for transfers between devices, from_root(): return lax.psum(block, axis)  586 us
    psum x8, waiting for transfers between devices, per_device(): reduce_row = lambda pending: lax.psum(pending, 'pcol')  281 us
    psum x1, waiting for transfers between devices, per_device(): totals = lax.psum(partial_rows, 'pcol')  77 us
    dot_general x8, matrix products, advance(): update = jnp.einsum('itc,cr->itr', columns, solution, precision=highest)  32.1 us
    all_gather x1, waiting for transfers between devices, per_device(): row_factor = lax.all_gather(panel_factor, 'pcol', axis=0, tiled=True)  26.5 us
  transfers between devices with their start and end apart: 20, of which 20 were waited for; matrix products, arithmetic and copies ran while one was open for 3% of the time, Pallas kernels for 0%

commit v1 on v0

--- a/solution.py
+++ b/solution.py
@@ -9,7 +9,8 @@
 
 def from_root(block, axis, owner):
     block = jnp.where(lax.axis_index(axis) == owner, block, jnp.zeros_like(block))
-    return lax.psum(block, axis)
+    _bind_spans = lambda mine, bus_axis: jnp.sum(lax.all_gather(mine, bus_axis), axis=0)
+    return _bind_spans(block, axis)
 
 
 def per_device(panel, strip, factor, inv_diag, rhs):

time: 1150 us -> 760 us (0.66)
  waiting for transfers between devices: 972 us -> 587 us
  other arithmetic: 41.2 us -> 54.6 us
    psum x10 -> x0, waiting for transfers between devices: 586 us -> none  [from_root(): return lax.psum(block, axis)]
    all_gather x0 -> x10, waiting for transfers between devices: none -> 274 us  [from_root(): lax.all_gather(mine, bus_axis)]
    psum x1, waiting for transfers between devices: 77 us -> 0.02 us  [per_device(): totals = lax.psum(partial_rows, 'pcol')]
    reduce_sum x0 -> x10, other arithmetic: none -> 13.4 us  [from_root(): jnp.sum(lax.all_gather(mine, bus_axis), axis=0)]
  transfers between devices with their start and end apart: 20 -> 20, of which waited for: 20 -> 19; matrix products, arithmetic and copies ran while one was open for 3% -> 8% of each run, Pallas kernels for 0% -> 0%
where the time goes in v1:
time: 760 us; the launch traced here: 758 us
  waiting for transfers between devices  587 us (77%)
  other arithmetic  54.6 us (7%)
  matrix products  49.9 us (7%)
  local copies, waits for them, and re-layouts  39.8 us (5%)
  between operations  15.4 us (2%)
  blocking collectives  11 us (1%)
    psum x8, waiting for transfers between devices, per_device(): reduce_row = lambda pending: lax.psum(pending, 'pcol')  289 us
    all_gather x10, waiting for transfers between devices, from_root(): lax.all_gather(mine, bus_axis)  274 us
    dot_general x8, matrix products, advance(): update = jnp.einsum('itc,cr->itr', columns, solution, precision=highest)  24.9 us
    dynamic_slice x8, local copies, waits for them, and re-layouts, advance(): lax.dynamic_index_in_dim(factor, sweep_step // grid_cols, 2, keepdims=False)  21.5 us
    all_gather x1, waiting for transfers between devices, per_device(): row_factor = lax.all_gather(panel_factor, 'pcol', axis=0, tiled=True)  21.4 us
    dot_general x8, matrix products, advance(): solution = jnp.dot(diag_inverse, residue, precision=highest)  15.4 us
  transfers between devices with their start and end apart: 20, of which 19 were waited for; matrix products, arithmetic and copies ran while one was open for 8% of the time, Pallas kernels for 0%

profile of v1, /device:TPU:0, one launch (start us, length us, event | category | flops | bytes accessed | tf_op | source)
XLA Modules:
  0.0 758.3 jit_solution(8417935347485946068)
XLA Ops:
  8.0 1.5 slice_select_fusion
  9.5 553.3 %while.19 = (s32[]{:T(128)}, f32[16,128,256]{2,1,0:T(8,128)}, f32[8,128,256]{2,1,0:T(8,128)}, s32[]{:T(128)}, f32[16,128,2,128]{3,2,1,0:T(2,128)}, /*index=5*/f3...) while((s32[]{:T(128)}, f32[16,128,256]{2,1,0:T(8,128)}, ...), condition=%wide.region_6.7_spmd.clone, body=%wide.region_3.6_spmd.clone.sunk | while | flops 857538624 | bytes 18154100 | solution.py:79
  10.5 40.0 %all-reduce.5.cloned.1.call-done = f32[128,256]{1,0:T(8,128)} async-done(((f32[128,256]{1,0:T(8,128)}), f32[128,256]{1,0:T(8,128)}) %all-reduce.5.cloned.1.call-update) | async-done | bytes 131088 | tf_op jit(solution)/shard_map/while/body/eval_jaxpr/psum | solution.py:58
  50.5 1.9 convolution_select_fusion.4
  52.5 2.7 constant_dynamic-slice_fusion.3
  55.2 21.0 %all-gather.16.cloned.1.call-done = f32[1024,256]{1,0:T(8,128)} async-done(((f32[128,256]{1,0:T(8,128)}), f32[1024,256]{1,0:T(8,128)}) %all-gather.16.cloned.1.call-update) | async-done | bytes 1048592 | tf_op jit(solution)/shard_map/while/body/eval_jaxpr/all_gather | solution.py:12
  76.1 1.3 reduce_sum.39
  78.1 3.1 select_add_fusion.2
  81.2 1.8 broadcast_select_fusion.3
  83.8 35.7 %all-reduce.5.cloned.1.call-done = f32[128,256]{1,0:T(8,128)} async-done(((f32[128,256]{1,0:T(8,128)}), f32[128,256]{1,0:T(8,128)}) %all-reduce.5.cloned.1.call-update) | async-done | bytes 131088 | tf_op jit(solution)/shard_map/while/body/eval_jaxpr/psum | solution.py:58
  119.5 1.9 convolution_select_fusion.4
  121.5 2.7 constant_dynamic-slice_fusion.3
  124.2 20.8 %all-gather.16.cloned.1.call-done = f32[1024,256]{1,0:T(8,128)} async-done(((f32[128,256]{1,0:T(8,128)}), f32[1024,256]{1,0:T(8,128)}) %all-gather.16.cloned.1.call-update) | async-done | bytes 1048592 | tf_op jit(solution)/shard_map/while/body/eval_jaxpr/all_gather | solution.py:12
  147.0 3.1 select_add_fusion.2
  150.1 1.8 broadcast_select_fusion.3
  152.7 35.4 %all-reduce.5.cloned.1.call-done = f32[128,256]{1,0:T(8,128)} async-done(((f32[128,256]{1,0:T(8,128)}), f32[128,256]{1,0:T(8,128)}) %all-reduce.5.cloned.1.call-update) | async-done | bytes 131088 | tf_op jit(solution)/shard_map/while/body/eval_jaxpr/psum | solution.py:58
  188.1 1.9 convolution_select_fusion.4
  190.0 2.7 constant_dynamic-slice_fusion.3
  192.7 20.8 %all-gather.16.cloned.1.call-done = f32[1024,256]{1,0:T(8,128)} async-done(((f32[128,256]{1,0:T(8,128)}), f32[1024,256]{1,0:T(8,128)}) %all-gather.16.cloned.1.call-update) | async-done | bytes 1048592 | tf_op jit(solution)/shard_map/while/body/eval_jaxpr/all_gather | solution.py:12
  215.5 3.1 select_add_fusion.2
  218.6 1.8 broadcast_select_fusion.3
  221.2 35.7 %all-reduce.5.cloned.1.call-done = f32[128,256]{1,0:T(8,128)} async-done(((f32[128,256]{1,0:T(8,128)}), f32[128,256]{1,0:T(8,128)}) %all-reduce.5.cloned.1.call-update) | async-done | bytes 131088 | tf_op jit(solution)/shard_map/while/body/eval_jaxpr/psum | solution.py:58
  257.0 1.9 convolution_select_fusion.4
  258.9 2.7 constant_dynamic-slice_fusion.3
  261.6 21.0 %all-gather.16.cloned.1.call-done = f32[1024,256]{1,0:T(8,128)} async-done(((f32[128,256]{1,0:T(8,128)}), f32[1024,256]{1,0:T(8,128)}) %all-gather.16.cloned.1.call-update) | async-done | bytes 1048592 | tf_op jit(solution)/shard_map/while/body/eval_jaxpr/all_gather | solution.py:12
  284.5 3.1 select_add_fusion.2
  287.7 1.8 broadcast_select_fusion.3
  290.2 35.7 %all-reduce.5.cloned.1.call-done = f32[128,256]{1,0:T(8,128)} async-done(((f32[128,256]{1,0:T(8,128)}), f32[128,256]{1,0:T(8,128)}) %all-reduce.5.cloned.1.call-update) | async-done | bytes 131088 | tf_op jit(solution)/shard_map/while/body/eval_jaxpr/psum | solution.py:58
  325.9 1.9 convolution_select_fusion.4
  327.9 2.7 constant_dynamic-slice_fusion.3
  330.6 20.9 %all-gather.16.cloned.1.call-done = f32[1024,256]{1,0:T(8,128)} async-done(((f32[128,256]{1,0:T(8,128)}), f32[1024,256]{1,0:T(8,128)}) %all-gather.16.cloned.1.call-update) | async-done | bytes 1048592 | tf_op jit(solution)/shard_map/while/body/eval_jaxpr/all_gather | solution.py:12
  353.4 3.1 select_add_fusion.2
  356.5 1.8 broadcast_select_fusion.3
  359.1 35.7 %all-reduce.5.cloned.1.call-done = f32[128,256]{1,0:T(8,128)} async-done(((f32[128,256]{1,0:T(8,128)}), f32[128,256]{1,0:T(8,128)}) %all-reduce.5.cloned.1.call-update) | async-done | bytes 131088 | tf_op jit(solution)/shard_map/while/body/eval_jaxpr/psum | solution.py:58
  394.8 1.9 convolution_select_fusion.4
  396.8 2.7 constant_dynamic-slice_fusion.3
  399.5 20.8 %all-gather.16.cloned.1.call-done = f32[1024,256]{1,0:T(8,128)} async-done(((f32[128,256]{1,0:T(8,128)}), f32[1024,256]{1,0:T(8,128)}) %all-gather.16.cloned.1.call-update) | async-done | bytes 1048592 | tf_op jit(solution)/shard_map/while/body/eval_jaxpr/all_gather | solution.py:12
  422.3 3.1 select_add_fusion.2
  425.4 1.8 broadcast_select_fusion.3
  428.0 35.7 %all-reduce.5.cloned.1.call-done = f32[128,256]{1,0:T(8,128)} async-done(((f32[128,256]{1,0:T(8,128)}), f32[128,256]{1,0:T(8,128)}) %all-reduce.5.cloned.1.call-update) | async-done | bytes 131088 | tf_op jit(solution)/shard_map/while/body/eval_jaxpr/psum | solution.py:58
  463.7 1.9 convolution_select_fusion.4
  465.7 2.7 constant_dynamic-slice_fusion.3
  468.4 20.8 %all-gather.16.cloned.1.call-done = f32[1024,256]{1,0:T(8,128)} async-done(((f32[128,256]{1,0:T(8,128)}), f32[1024,256]{1,0:T(8,128)}) %all-gather.16.cloned.1.call-update) | async-done | bytes 1048592 | tf_op jit(solution)/shard_map/while/body/eval_jaxpr/all_gather | solution.py:12
  491.1 3.1 select_add_fusion.2
  494.3 1.8 broadcast_select_fusion.3
  496.8 35.4 %all-reduce.5.cloned.1.call-done = f32[128,256]{1,0:T(8,128)} async-done(((f32[128,256]{1,0:T(8,128)}), f32[128,256]{1,0:T(8,128)}) %all-reduce.5.cloned.1.call-update) | async-done | bytes 131088 | tf_op jit(solution)/shard_map/while/body/eval_jaxpr/psum | solution.py:58
  532.2 1.9 convolution_select_fusion.4
  534.2 2.7 constant_dynamic-slice_fusion.3
  536.9 20.8 %all-gather.16.cloned.1.call-done = f32[1024,256]{1,0:T(8,128)} async-done(((f32[128,256]{1,0:T(8,128)}), f32[1024,256]{1,0:T(8,128)}) %all-gather.16.cloned.1.call-update) | async-done | bytes 1048592 | tf_op jit(solution)/shard_map/while/body/eval_jaxpr/all_gather | solution.py:12
  559.7 3.1 select_add_fusion.2
  564.0 102.6 %all-gather.10.cloned.1.call-done = f32[32,128,128]{2,1,0:T(8,128)} async-done(((f32[1,128,128]{2,1,0:T(8,128)}), f32[32,128,128]{2,1,0:T(8,128)}) %all-gather.10.cloned.1.call-update) | async-done | bytes 2097168 | tf_op jit(solution)/shard_map/all_gather | solution.py:12
  666.7 1.7 reduce_sum.35
  668.5 11.7 %cholesky.19 = f32[128,128]{1,0:T(8,128)S(1)} custom-call(f32[128,128]{1,0:T(8,128)S(1)} %fusion.13), custom_call_target="Cholesky" | custom-call | tf_op jit(solution)/shard_map/jit(cholesky)/cholesky | solution.py:31
  681.5 9.8 %custom-call.7 = f32[1,128,128]{1,2,0:T(8,128)S(1)} custom-call(f32[1,128,128]{2,1,0:T(8,128)S(1)} %get-tuple-element.278), custom_call_target="InvertDiagBlocksLowerTriangular" | custom-call | tf_op jit(solution)/shard_map/jit(_solve_triangular)/triangular_solve | solution.py:32
  693.1 2.6 sub.72
  696.7 2.0 gather_fusion.1
  698.7 21.4 %all-gather.12.cloned.1.call-done = f32[16,128,128]{2,1,0:T(8,128)} async-done(((f32[4,128,128]{2,1,0:T(8,128)}), f32[16,128,128]{2,1,0:T(8,128)}) %all-gather.12.cloned.1.call-update) | async-done | bytes 1048592 | tf_op jit(solution)/shard_map/all_gather | solution.py:41
  720.1 1.4 broadcast_select_fusion.1
  721.5 11.0 %all_gather.40 = f32[8,128,128]{2,1,0:T(8,128)} all-gather(f32[1,128,128]{2,1,0:T(8,128)S(1)} %constant_dynamic-slice_fusion.1), channel_id=1, replica_groups=mesh['prow'=8,'pcol'=4] {'prow'}, dimensions={0}, use_global_device_ids=true | all-gather | bytes 589824 | tf_op jit(solution)/shard_map/all_gather | solution.py:48
  732.5 1.6 gather_fusion
  734.1 3.4 copy_subtract_fusion
  737.5 2.9 copy.23
  740.5 4.7 all-gather.14.cloned.1.call-done
  746.5 4.7 select_select_fusion
  (90 shorter events, 27.2 us)
Async XLA Ops:
  9.5 41.0 %all-reduce.5.cloned.1.call-start = ((), (), s32[]{:S(2)}) async-start(), calls=%async_computation.4 | async-start | bytes 262144 | tf_op jit(solution)/shard_map/while/body/eval_jaxpr/psum | solution.py:58
  10.4 65.7 %all-gather.16.cloned.1.call-start = ((), (), s32[]{:S(2)}) async-start(), calls=%async_computation.5 | async-start | bytes 1179648 | tf_op jit(solution)/shard_map/while/body/eval_jaxpr/all_gather | solution.py:12
  81.2 38.3 %all-reduce.5.cloned.1.call-start = ((), (), s32[]{:S(2)}) async-start(), calls=%async_computation.4 | async-start | bytes 262144 | tf_op jit(solution)/shard_map/while/body/eval_jaxpr/psum | solution.py:58
  83.7 61.3 %all-gather.16.cloned.1.call-start = ((), (), s32[]{:S(2)}) async-start(), calls=%async_computation.5 | async-start | bytes 1179648 | tf_op jit(solution)/shard_map/while/body/eval_jaxpr/all_gather | solution.py:12
  150.1 38.0 %all-reduce.5.cloned.1.call-start = ((), (), s32[]{:S(2)}) async-start(), calls=%async_computation.4 | async-start | bytes 262144 | tf_op jit(solution)/shard_map/while/body/eval_jaxpr/psum | solution.py:58
  152.6 61.0 %all-gather.16.cloned.1.call-start = ((), (), s32[]{:S(2)}) async-start(), calls=%async_computation.5 | async-start | bytes 1179648 | tf_op jit(solution)/shard_map/while/body/eval_jaxpr/all_gather | solution.py:12
  218.6 38.3 %all-reduce.5.cloned.1.call-start = ((), (), s32[]{:S(2)}) async-start(), calls=%async_computation.4 | async-start | bytes 262144 | tf_op jit(solution)/shard_map/while/body/eval_jaxpr/psum | solution.py:58
  221.2 61.4 %all-gather.16.cloned.1.call-start = ((), (), s32[]{:S(2)}) async-start(), calls=%async_computation.5 | async-start | bytes 1179648 | tf_op jit(solution)/shard_map/while/body/eval_jaxpr/all_gather | solution.py:12
  287.7 38.3 %all-reduce.5.cloned.1.call-start = ((), (), s32[]{:S(2)}) async-start(), calls=%async_computation.4 | async-start | bytes 262144 | tf_op jit(solution)/shard_map/while/body/eval_jaxpr/psum | solution.py:58
  290.2 61.3 %all-gather.16.cloned.1.call-start = ((), (), s32[]{:S(2)}) async-start(), calls=%async_computation.5 | async-start | bytes 1179648 | tf_op jit(solution)/shard_map/while/body/eval_jaxpr/all_gather | solution.py:12
  356.5 38.3 %all-reduce.5.cloned.1.call-start = ((), (), s32[]{:S(2)}) async-start(), calls=%async_computation.4 | async-start | bytes 262144 | tf_op jit(solution)/shard_map/while/body/eval_jaxpr/psum | solution.py:58
  359.0 61.3 %all-gather.16.cloned.1.call-start = ((), (), s32[]{:S(2)}) async-start(), calls=%async_computation.5 | async-start | bytes 1179648 | tf_op jit(solution)/shard_map/while/body/eval_jaxpr/all_gather | solution.py:12
  425.4 38.3 %all-reduce.5.cloned.1.call-start = ((), (), s32[]{:S(2)}) async-start(), calls=%async_computation.4 | async-start | bytes 262144 | tf_op jit(solution)/shard_map/while/body/eval_jaxpr/psum | solution.py:58
  427.9 61.3 %all-gather.16.cloned.1.call-start = ((), (), s32[]{:S(2)}) async-start(), calls=%async_computation.5 | async-start | bytes 1179648 | tf_op jit(solution)/shard_map/while/body/eval_jaxpr/all_gather | solution.py:12
  494.3 38.0 %all-reduce.5.cloned.1.call-start = ((), (), s32[]{:S(2)}) async-start(), calls=%async_computation.4 | async-start | bytes 262144 | tf_op jit(solution)/shard_map/while/body/eval_jaxpr/psum | solution.py:58
  496.8 61.0 %all-gather.16.cloned.1.call-start = ((), (), s32[]{:S(2)}) async-start(), calls=%async_computation.5 | async-start | bytes 1179648 | tf_op jit(solution)/shard_map/while/body/eval_jaxpr/all_gather | solution.py:12
  562.8 103.9 %all-gather.10.cloned.1.call-start = ((), (), s32[]{:S(2)}) async-start(), calls=%async_computation | async-start | bytes 2162688 | tf_op jit(solution)/shard_map/all_gather | solution.py:12
  563.4 129.7 %all-reduce.3.cloned.1.call-start = ((), (), s32[]{:S(2)}) async-start(), calls=%async_computation.2 | async-start | bytes 4194304 | tf_op jit(solution)/shard_map/psum | solution.py:83
  563.4 128.3 %copy-start.1 = (f32[4,128,128]{2,1,0:T(8,128)S(1)}, f32[4,128,128]{2,1,0:T(8,128)}, u32[]{:S(2)}) copy-start(f32[4,128,128]{2,1,0:T(8,128)} %param.7) | copy-start | bytes 786436
  564.0 156.2 %all-gather.12.cloned.1.call-start = ((), (), s32[]{:S(2)}) async-start(), calls=%async_computation.1 | async-start | bytes 1310720 | tf_op jit(solution)/shard_map/all_gather | solution.py:41
  693.0 52.2 %all-gather.14.cloned.1.call-start = ((), (), s32[]{:S(2)}) async-start(), calls=%async_computation.3 | async-start | bytes 1179648 | tf_op jit(solution)/shard_map/all_gather | solution.py:12
  693.0 3.6 copy-start
Sparse Core Ops, SparseCore 0:
  13.3 37.1 all-reduce.4
  53.0 23.1 all-gather.15
  85.0 34.4 all-reduce.4
  121.8 23.1 all-gather.15
  153.6 34.4 all-reduce.4
  190.4 23.1 all-gather.15
  222.5 34.4 all-reduce.4
  259.4 23.1 all-gather.15
  291.5 34.3 all-reduce.4
  328.2 23.1 all-gather.15
  360.3 34.4 all-reduce.4
  397.1 23.1 all-gather.15
  429.2 34.4 all-reduce.4
  466.0 23.1 all-gather.15
  497.8 34.4 all-reduce.4
  534.6 23.1 all-gather.15
  566.8 89.8 all-reduce.2
  693.1 27.0 all-gather.11
  722.2 22.9 all-gather.13
Sparse Core Ops, SparseCore 1:
  566.2 100.4 all-gather.9
